TPU v7x, 32 devices: a whole 2x2x4 slice. The times are simulated.
32 devices in a mesh: seq: 8 (over y, x, core), dp: 4 (over z).
Axes of the slice: x: 2, y: 2, z: 4, core: 2. Of those that a mesh axis runs over, the one named last changes fastest.
Arguments:
- query: bfloat16 [4, 1536, 1280], P('dp', 'seq'), may hold values from -52 to 52, as said below
- keys: bfloat16 [4, 1536, 1280], P('dp', 'seq'), may hold values from -6 to 6, as said below
- values: bfloat16 [4, 1536, 1280], P('dp', 'seq'), may hold values from -6 to 6
- attn: bfloat16 [4, 1536, 1280], P('dp', 'seq'), may hold values from -6 to 6
- d_block: bfloat16 [4, 1536, 1280], P('dp', 'seq'), may hold values from -6 to 6
- w_out: bfloat16 [1280, 1280], P('dp'), may hold values from -0.15625 to 0.15625
Outputs:
- d_query: bfloat16 [4, 1536, 1280], P('dp', 'seq')
- d_keys: bfloat16 [4, 1536, 1280], P('dp', 'seq')
- d_values: bfloat16 [4, 1536, 1280], P('dp', 'seq')
- d_weight: float32 [1280, 1280], P('dp')
Inputs may be any that keep to these rules, and one draw needn't show every extreme that they name: Some query patches may lie along the sum of two keys of the same video. keys has entries of order one.
All inputs are finite; a program needn't handle non-finite values.
Results may differ from a plain program's by a relative error of at most 0.0058.
Values may be sent and summed in bfloat16 or wider, within the bound.
A program may use at most 64 MiB of HBM per device.

v0:
```python
import jax
import jax.numpy as jnp
from jax import lax
from jax.sharding import PartitionSpec as P

HEAD_DIM = 80


def head_backward(query_h, keys_h, values_h, dout_h, delta_h):
    patch_total = query_h.shape[0]
    block_rows = min(512, patch_total)
    while patch_total % block_rows != 0:
        block_rows = block_rows // 2
    block_total = patch_total // block_rows
    score_scale = HEAD_DIM ** (-0.5)
    contract_last = (((1,), (1,)), ((), ()))
    contract_first = (((0,), (0,)), ((), ()))

    def one_block(carry, inputs):
        keys_grad, values_grad = carry
        query_block, dout_block, delta_block = inputs
        scores = (
            lax.dot_general(query_block, keys_h, contract_last, preferred_element_type=jnp.float32)
            * score_scale
        )
        row_max = jnp.max(scores, axis=1, keepdims=True)
        lse = row_max + jnp.log(jnp.sum(jnp.exp(scores - row_max), axis=1, keepdims=True))
        probs = jnp.exp(scores - lse)
        probs_low = probs.astype(jnp.bfloat16)
        values_grad = values_grad + lax.dot_general(
            probs_low, dout_block, contract_first, preferred_element_type=jnp.float32
        )
        d_probs = lax.dot_general(
            dout_block, values_h, contract_last, preferred_element_type=jnp.float32
        )
        d_scores = (score_scale * probs * (d_probs - delta_block[:, None])).astype(jnp.bfloat16)
        query_grad = jnp.dot(d_scores, keys_h, preferred_element_type=jnp.float32)
        keys_grad = keys_grad + lax.dot_general(
            d_scores, query_block, contract_first, preferred_element_type=jnp.float32
        )
        return ((keys_grad, values_grad), query_grad.astype(jnp.bfloat16))

    empty = jnp.zeros((patch_total, HEAD_DIM), jnp.float32)
    blocked = (
        query_h.reshape(block_total, block_rows, HEAD_DIM),
        dout_h.reshape(block_total, block_rows, HEAD_DIM),
        delta_h.reshape(block_total, block_rows),
    )
    (keys_grad, values_grad), query_blocks = lax.scan(one_block, (empty, empty), blocked)
    return (
        query_blocks.reshape(patch_total, HEAD_DIM),
        keys_grad.astype(jnp.bfloat16),
        values_grad.astype(jnp.bfloat16),
    )


def body(query, keys, values, attn, d_block, w_out):
    seq_count = lax.axis_size("seq")
    dp_count = lax.axis_size("dp")
    tok_rows = query.shape[1]
    features = query.shape[2]
    head_here = features // HEAD_DIM // seq_count
    grad_y = d_block.reshape(tok_rows, features)
    attn_rows = attn.reshape(tok_rows, features)
    d_out = lax.dot_general(
        grad_y,
        lax.all_gather(w_out, "dp", axis=0, tiled=True),
        (((1,), (1,)), ((), ())),
        preferred_element_type=jnp.float32,
    ).astype(jnp.bfloat16)

    def split_heads(array):
        return array.reshape(tok_rows, seq_count, head_here, HEAD_DIM)

    query_all, keys_all, values_all, dout_all, output_all = (
        lax.all_to_all(split_heads(query), "seq", split_axis=1, concat_axis=0, tiled=True),
        lax.all_to_all(split_heads(keys), "seq", split_axis=1, concat_axis=0, tiled=True),
        lax.all_to_all(split_heads(values), "seq", split_axis=1, concat_axis=0, tiled=True),
        lax.all_to_all(split_heads(d_out), "seq", split_axis=1, concat_axis=0, tiled=True),
        lax.all_to_all(split_heads(attn_rows), "seq", split_axis=1, concat_axis=0, tiled=True),
    )
    row_terms = jnp.sum(dout_all.astype(jnp.float32) * output_all.astype(jnp.float32), axis=3)
    query_list = []
    keys_list = []
    values_list = []
    for head in range(head_here):
        gradient = head_backward(
            query_all[:, 0, head],
            keys_all[:, 0, head],
            values_all[:, 0, head],
            dout_all[:, 0, head],
            row_terms[:, 0, head],
        )
        query_list.append(gradient[0])
        keys_list.append(gradient[1])
        values_list.append(gradient[2])
    query_heads = jnp.stack(query_list, axis=1)[:, None]
    keys_heads = jnp.stack(keys_list, axis=1)[:, None]
    values_heads = jnp.stack(values_list, axis=1)[:, None]
    query_back, keys_back, values_back = (
        lax.all_to_all(query_heads, "seq", split_axis=0, concat_axis=1, tiled=True),
        lax.all_to_all(keys_heads, "seq", split_axis=0, concat_axis=1, tiled=True),
        lax.all_to_all(values_heads, "seq", split_axis=0, concat_axis=1, tiled=True),
    )
    factor = 1.0 / float(dp_count * tok_rows * seq_count) ** 0.5
    contract_first = (((0,), (0,)), ((), ()))
    partial_rows = lax.psum_scatter(
        lax.dot_general(attn_rows, grad_y, contract_first, preferred_element_type=jnp.float32)
        * factor,
        "dp",
        scatter_dimension=0,
        tiled=True,
    )
    d_weight = lax.psum(partial_rows, "seq")
    shape_out = (1, tok_rows, features)
    return (
        query_back.reshape(shape_out),
        keys_back.reshape(shape_out),
        values_back.reshape(shape_out),
        d_weight,
    )


def solution(mesh):
    return jax.shard_map(
        body,
        mesh=mesh,
        in_specs=(
            P("dp", "seq", None),
            P("dp", "seq", None),
            P("dp", "seq", None),
            P("dp", "seq", None),
            P("dp", "seq", None),
            P("dp", None),
        ),
        out_specs=(P("dp", "seq", None), P("dp", "seq", None), P("dp", "seq", None), P("dp", None)),
        check_vma=False,
    )
```

profile of v0, /device:TPU:0, one launch (start us, length us, event | category | flops | bytes accessed | tf_op | source)
XLA Modules:
  0.0 278.9 jit_solution(8899856098852248446)
XLA Ops:
  10.0 5.2 %all-to-all-start = ((bf16[192,8,2,80]{0,3,2,1:T(8,128)(2,1)}), bf16[192,8,2,80]{0,3,2,1:T(8,128)(2,1)S(1)}, u32[]{:S(2)}, u32[]{:S(2)}) async-start(bf16[192,8,2,80]{0,3,2,1:T(8,128)(2,1)} %bitcast), calls=%async_computation | async-start | bytes 1310720 | tf_op jit(solution)/shard_map/all_to_all | solution.py:76
  15.3 3.8 %convolution_multiply_fusion.2 = f32[1280,1280]{1,0:T(8,128)} fusion(bf16[1,192,1280]{2,1,0:T(8,128)(2,1)S(1)} %copy-done.8, bf16[1,192,1280]{2,1,0:T(8,128)(2,1)S(1)} %copy-done), kind=kOutput, calls=%fused_computation.54 | convolution fusion | flops 630784000 | bytes 7536640 | tf_op jit(solution)/shard_map/dot_general | solution.py:108
  26.3 4.2 %all-to-all-start.1 = ((bf16[192,8,2,80]{0,3,2,1:T(8,128)(2,1)}), bf16[192,8,2,80]{0,3,2,1:T(8,128)(2,1)}, u32[]{:S(2)}, u32[]{:S(2)}) async-start(bf16[192,8,2,80]{0,3,2,1:T(8,128)(2,1)} %bitcast.192), calls=%async_computation.1 | async-start | bytes 1310720 | tf_op jit(solution)/shard_map/all_to_all | solution.py:77
  34.5 7.2 %all-to-all-done.1 = bf16[192,8,2,80]{0,3,2,1:T(8,128)(2,1)} async-done(((bf16[192,8,2,80]{0,3,2,1:T(8,128)(2,1)}), bf16[192,8,2,80]{0,3,2,1:T(8,128)(2,1)}, u32[]{:S(2)}, u32[]{:S(2)}) %all-to-all-start.1) | async-done | bytes 491552 | tf_op jit(solution)/shard_map/all_to_all | solution.py:77
  41.7 4.2 %all-to-all-start.3 = ((bf16[192,8,2,80]{0,3,2,1:T(8,128)(2,1)}), bf16[192,8,2,80]{0,3,2,1:T(8,128)(2,1)}, u32[]{:S(2)}, u32[]{:S(2)}) async-start(bf16[192,8,2,80]{0,3,2,1:T(8,128)(2,1)} %bitcast.13), calls=%async_computation.3 | async-start | bytes 1310720 | tf_op jit(solution)/shard_map/all_to_all | solution.py:78
  50.7 6.4 %all-to-all-done.3 = bf16[192,8,2,80]{0,3,2,1:T(8,128)(2,1)} async-done(((bf16[192,8,2,80]{0,3,2,1:T(8,128)(2,1)}), bf16[192,8,2,80]{0,3,2,1:T(8,128)(2,1)}, u32[]{:S(2)}, u32[]{:S(2)}) %all-to-all-start.3) | async-done | bytes 491552 | tf_op jit(solution)/shard_map/all_to_all | solution.py:78
  57.0 2.3 copy.119
  59.3 2.4 all_to_all.107
  61.7 16.2 %all-gather.2.cloned.1.call-done = bf16[1280,1280]{1,0:T(8,128)(2,1)} async-done(((bf16[320,1280]{1,0:T(8,128)(2,1)}), bf16[1280,1280]{1,0:T(8,128)(2,1)}) %all-gather.2.cloned.1.call-update) | async-done | bytes 3276816 | tf_op jit(solution)/shard_map/all_gather | solution.py:67
  77.9 3.9 %convolution_convert_fusion.2 = bf16[192,1280]{1,0:T(8,128)(2,1)} fusion(bf16[1280,1280]{1,0:T(8,128)(2,1)} %all-gather.2.cloned.1.call-done, bf16[1,192,1280]{2,1,0:T(8,128)(2,1)S(1)} %copy-done), kind=kOutput, calls=%fused_computation.55 | convolution fusion | flops 629391360 | bytes 4259840 | tf_op jit(solution)/shard_map/dot_general | solution.py:65
  84.0 4.2 %all-to-all-start.2 = ((bf16[192,8,2,80]{0,3,2,1:T(8,128)(2,1)}), bf16[192,8,2,80]{0,3,2,1:T(8,128)(2,1)}, u32[]{:S(2)}, u32[]{:S(2)}) async-start(bf16[192,8,2,80]{0,3,2,1:T(8,128)(2,1)} %bitcast.193), calls=%async_computation.2 | async-start | bytes 1310720 | tf_op jit(solution)/shard_map/all_to_all | solution.py:79
  94.9 4.5 %all-to-all-done.2 = bf16[192,8,2,80]{0,3,2,1:T(8,128)(2,1)} async-done(((bf16[192,8,2,80]{0,3,2,1:T(8,128)(2,1)}), bf16[192,8,2,80]{0,3,2,1:T(8,128)(2,1)}, u32[]{:S(2)}, u32[]{:S(2)}) %all-to-all-start.2) | async-done | bytes 491552 | tf_op jit(solution)/shard_map/all_to_all | solution.py:79
  99.3 4.4 %all-to-all-start.4 = ((bf16[192,8,2,80]{0,3,2,1:T(8,128)(2,1)}), bf16[192,8,2,80]{0,3,2,1:T(8,128)(2,1)}, u32[]{:S(2)}, u32[]{:S(2)}) async-start(bf16[192,8,2,80]{0,3,2,1:T(8,128)(2,1)} %bitcast.190), calls=%async_computation.4 | async-start | bytes 1310720 | tf_op jit(solution)/shard_map/all_to_all | solution.py:80
  103.7 2.3 copy.117
  106.0 2.4 all_to_all.103
  112.1 2.6 all-to-all-done.4
  117.4 31.8 %while.30 = (s32[]{:T(128)}, f32[1536,80]{0,1:T(8,128)S(1)}, f32[1536,80]{0,1:T(8,128)S(1)}, bf16[3,512,80]{1,2,0:T(8,128)(2,1)S(1)}, bf16[3,512,80]{2,1,0:T(8,1...) while((s32[]{:T(128)}, f32[1536,80]{0,1:T(8,128)S(1)}, ...), condition=%wide.region_4.5_spmd.clone, body=%wide.region_1.4_spmd.clone.sunk | while | flops 638328320 | bytes 46932176 | solution.py:49
  121.3 2.8 %convolution_add_fusion.9 = f32[1536,80]{0,1:T(8,128)S(1)} fusion(f32[512,1536]{1,0:T(8,128)} %copy-done.1, f32[512]{0:T(512)S(1)} %log_add_fusion.4, f32[1536,80]{0,1:T(8,128)S(1)} %get-tuple-element.496, pred[]{:T(512)S(6)} %compare.6, bf16[3,512,80]{2,1,0:T(8,128)(2,1)} %get-tuple-element.511, s32[]{:T(128)} %get-tuple-element.494), kind=kOutput, calls=%fused_computation.7.clone.1 | convolution fusion | flops 127647744 | bytes 4262401 | tf_op jit(solution)/shard_map/while/body/eval_jaxpr/dot_general | solution.py:30
  131.9 2.8 %convolution_add_fusion.9 = f32[1536,80]{0,1:T(8,128)S(1)} fusion(f32[512,1536]{1,0:T(8,128)} %copy-done.1, f32[512]{0:T(512)S(1)} %log_add_fusion.4, f32[1536,80]{0,1:T(8,128)S(1)} %get-tuple-element.496, pred[]{:T(512)S(6)} %compare.6, bf16[3,512,80]{2,1,0:T(8,128)(2,1)} %get-tuple-element.511, s32[]{:T(128)} %get-tuple-element.494), kind=kOutput, calls=%fused_computation.7.clone.1 | convolution fusion | flops 127647744 | bytes 4262401 | tf_op jit(solution)/shard_map/while/body/eval_jaxpr/dot_general | solution.py:30
  142.5 2.8 %convolution_add_fusion.9 = f32[1536,80]{0,1:T(8,128)S(1)} fusion(f32[512,1536]{1,0:T(8,128)} %copy-done.1, f32[512]{0:T(512)S(1)} %log_add_fusion.4, f32[1536,80]{0,1:T(8,128)S(1)} %get-tuple-element.496, pred[]{:T(512)S(6)} %compare.6, bf16[3,512,80]{2,1,0:T(8,128)(2,1)} %get-tuple-element.511, s32[]{:T(128)} %get-tuple-element.494), kind=kOutput, calls=%fused_computation.7.clone.1 | convolution fusion | flops 127647744 | bytes 4262401 | tf_op jit(solution)/shard_map/while/body/eval_jaxpr/dot_general | solution.py:30
  150.0 29.2 %while.31 = (s32[]{:T(128)}, f32[1536,80]{0,1:T(8,128)S(1)}, f32[1536,80]{0,1:T(8,128)S(1)}, bf16[3,512,80]{1,2,0:T(8,128)(2,1)S(1)}, bf16[3,512,80]{2,1,0:T(8,1...) while((s32[]{:T(128)}, f32[1536,80]{0,1:T(8,128)S(1)}, ...), condition=%wide.region_8.9_spmd.clone, body=%wide.region_5.8_spmd.clone.sunk | while | flops 638328320 | bytes 48061684 | solution.py:49
  154.0 2.8 %convolution_add_fusion.11 = f32[1536,80]{0,1:T(8,128)S(1)} fusion(f32[512,1536]{1,0:T(8,128)} %copy-done.3, f32[512]{0:T(512)S(1)} %log_add_fusion.5, f32[1536,80]{0,1:T(8,128)S(1)} %get-tuple-element.463, pred[]{:T(512)S(6)} %compare.7, bf16[3,512,80]{2,1,0:T(8,128)(2,1)S(1)} %copy-done.7, s32[]{:T(128)} %get-tuple-element.461), kind=kOutput, calls=%fused_computation.34.clone.1 | convolution fusion | flops 127647744 | bytes 4261893 | tf_op jit(solution)/shard_map/while/body/eval_jaxpr/dot_general | solution.py:30
  163.8 2.8 %convolution_add_fusion.11 = f32[1536,80]{0,1:T(8,128)S(1)} fusion(f32[512,1536]{1,0:T(8,128)} %copy-done.3, f32[512]{0:T(512)S(1)} %log_add_fusion.5, f32[1536,80]{0,1:T(8,128)S(1)} %get-tuple-element.463, pred[]{:T(512)S(6)} %compare.7, bf16[3,512,80]{2,1,0:T(8,128)(2,1)S(1)} %copy-done.7, s32[]{:T(128)} %get-tuple-element.461), kind=kOutput, calls=%fused_computation.34.clone.1 | convolution fusion | flops 127647744 | bytes 4261893 | tf_op jit(solution)/shard_map/while/body/eval_jaxpr/dot_general | solution.py:30
  173.5 2.8 %convolution_add_fusion.11 = f32[1536,80]{0,1:T(8,128)S(1)} fusion(f32[512,1536]{1,0:T(8,128)} %copy-done.3, f32[512]{0:T(512)S(1)} %log_add_fusion.5, f32[1536,80]{0,1:T(8,128)S(1)} %get-tuple-element.463, pred[]{:T(512)S(6)} %compare.7, bf16[3,512,80]{2,1,0:T(8,128)(2,1)S(1)} %copy-done.7, s32[]{:T(128)} %get-tuple-element.461), kind=kOutput, calls=%fused_computation.34.clone.1 | convolution fusion | flops 127647744 | bytes 4261893 | tf_op jit(solution)/shard_map/while/body/eval_jaxpr/dot_general | solution.py:30
  182.1 3.5 %all-to-all-start.7 = ((bf16[1536,1,2,80]{3,2,1,0:T(2,128)(2,1)}), bf16[1536,1,2,80]{3,2,1,0:T(2,128)(2,1)S(1)}, u32[]{:S(2)}, u32[]{:S(2)}) async-start(bf16[1536,1,2,80]{3,2,1,0:T(2,128)(2,1)} %copy.137), calls=%async_computation.7 | async-start | bytes 1572864 | tf_op jit(solution)/shard_map/all_to_all | solution.py:103
  187.6 10.6 %all-to-all-done.7 = bf16[1536,1,2,80]{3,2,1,0:T(2,128)(2,1)S(1)} async-done(((bf16[1536,1,2,80]{3,2,1,0:T(2,128)(2,1)}), bf16[1536,1,2,80]{3,2,1,0:T(2,128)(2,1)S(1)}, u32[]{:S(2)}, u32[]{:S(2)}) %all-to-all-start.7) | async-done | bytes 491552 | tf_op jit(solution)/shard_map/all_to_all | solution.py:103
  198.2 3.5 %all-to-all-start.6 = ((bf16[1536,1,2,80]{3,2,1,0:T(2,128)(2,1)}), bf16[1536,1,2,80]{3,2,1,0:T(2,128)(2,1)S(1)}, u32[]{:S(2)}, u32[]{:S(2)}) async-start(bf16[1536,1,2,80]{3,2,1,0:T(2,128)(2,1)} %copy.135), calls=%async_computation.6 | async-start | bytes 1572864 | tf_op jit(solution)/shard_map/all_to_all | solution.py:102
  205.5 10.5 %all-to-all-done.6 = bf16[1536,1,2,80]{3,2,1,0:T(2,128)(2,1)S(1)} async-done(((bf16[1536,1,2,80]{3,2,1,0:T(2,128)(2,1)}), bf16[1536,1,2,80]{3,2,1,0:T(2,128)(2,1)S(1)}, u32[]{:S(2)}, u32[]{:S(2)}) %all-to-all-start.6) | async-done | bytes 491552 | tf_op jit(solution)/shard_map/all_to_all | solution.py:102
  215.9 3.6 %all-to-all-start.5 = ((bf16[1536,1,2,80]{3,2,1,0:T(2,128)(2,1)}), bf16[1536,1,2,80]{3,2,1,0:T(2,128)(2,1)S(1)}, u32[]{:S(2)}, u32[]{:S(2)}) async-start(bf16[1536,1,2,80]{3,2,1,0:T(2,128)(2,1)} %copy.132), calls=%async_computation.5 | async-start | bytes 1572864 | tf_op jit(solution)/shard_map/all_to_all | solution.py:101
  225.7 6.2 %all-to-all-done.5 = bf16[1536,1,2,80]{3,2,1,0:T(2,128)(2,1)S(1)} async-done(((bf16[1536,1,2,80]{3,2,1,0:T(2,128)(2,1)}), bf16[1536,1,2,80]{3,2,1,0:T(2,128)(2,1)S(1)}, u32[]{:S(2)}, u32[]{:S(2)}) %all-to-all-start.5) | async-done | bytes 491552 | tf_op jit(solution)/shard_map/all_to_all | solution.py:101
  233.9 35.8 %all-reduce.2.cloned.1.call-done = f32[320,1280]{1,0:T(8,128)} async-done(((f32[320,1280]{1,0:T(8,128)}), f32[320,1280]{1,0:T(8,128)}) %all-reduce.2.cloned.1.call-update) | async-done | bytes 1638416 | tf_op jit(solution)/shard_map/psum | solution.py:114
  269.7 2.7 copy.174
  (150 shorter events, 94.8 us)
Async XLA Ops:
  7.2 8.1 %copy-start = (bf16[1,192,1280]{2,1,0:T(8,128)(2,1)S(1)}, bf16[1,192,1280]{2,1,0:T(8,128)(2,1)}, u32[]{:S(2)}) copy-start(bf16[1,192,1280]{2,1,0:T(8,128)(2,1)} %param.14) | copy-start | bytes 1474564
  7.2 8.1 %copy-start.8 = (bf16[1,192,1280]{2,1,0:T(8,128)(2,1)S(1)}, bf16[1,192,1280]{2,1,0:T(8,128)(2,1)}, u32[]{:S(2)}) copy-start(bf16[1,192,1280]{2,1,0:T(8,128)(2,1)} %param.13) | copy-start | bytes 1474564
  7.2 70.7 %all-gather.2.cloned.1.call-start = ((), (), s32[]{:S(2)}) async-start(), calls=%async_computation.9 | async-start | bytes 4096000 | tf_op jit(solution)/shard_map/all_gather | solution.py:67
  10.0 16.3 %all-to-all-start = ((bf16[192,8,2,80]{0,3,2,1:T(8,128)(2,1)}), bf16[192,8,2,80]{0,3,2,1:T(8,128)(2,1)S(1)}, u32[]{:S(2)}, u32[]{:S(2)}) async-start(bf16[192,8,2,80]{0,3,2,1:T(8,128)(2,1)} %bitcast), calls=%async_computation | async-start | bytes 1310720 | tf_op jit(solution)/shard_map/all_to_all | solution.py:76
  15.2 186.6 %reduce-scatter.2.cloned.1.call-start = ((), (), s32[]{:S(2)}) async-start(), calls=%async_computation.10 | async-start | bytes 8192000 | tf_op jit(solution)/shard_map/reduce_scatter | solution.py:107
  26.3 15.3 %all-to-all-start.1 = ((bf16[192,8,2,80]{0,3,2,1:T(8,128)(2,1)}), bf16[192,8,2,80]{0,3,2,1:T(8,128)(2,1)}, u32[]{:S(2)}, u32[]{:S(2)}) async-start(bf16[192,8,2,80]{0,3,2,1:T(8,128)(2,1)} %bitcast.192), calls=%async_computation.1 | async-start | bytes 1310720 | tf_op jit(solution)/shard_map/all_to_all | solution.py:77
  41.7 15.3 %all-to-all-start.3 = ((bf16[192,8,2,80]{0,3,2,1:T(8,128)(2,1)}), bf16[192,8,2,80]{0,3,2,1:T(8,128)(2,1)}, u32[]{:S(2)}, u32[]{:S(2)}) async-start(bf16[192,8,2,80]{0,3,2,1:T(8,128)(2,1)} %bitcast.13), calls=%async_computation.3 | async-start | bytes 1310720 | tf_op jit(solution)/shard_map/all_to_all | solution.py:78
  84.0 15.4 %all-to-all-start.2 = ((bf16[192,8,2,80]{0,3,2,1:T(8,128)(2,1)}), bf16[192,8,2,80]{0,3,2,1:T(8,128)(2,1)}, u32[]{:S(2)}, u32[]{:S(2)}) async-start(bf16[192,8,2,80]{0,3,2,1:T(8,128)(2,1)} %bitcast.193), calls=%async_computation.2 | async-start | bytes 1310720 | tf_op jit(solution)/shard_map/all_to_all | solution.py:79
  99.3 15.3 %all-to-all-start.4 = ((bf16[192,8,2,80]{0,3,2,1:T(8,128)(2,1)}), bf16[192,8,2,80]{0,3,2,1:T(8,128)(2,1)}, u32[]{:S(2)}, u32[]{:S(2)}) async-start(bf16[192,8,2,80]{0,3,2,1:T(8,128)(2,1)} %bitcast.190), calls=%async_computation.4 | async-start | bytes 1310720 | tf_op jit(solution)/shard_map/all_to_all | solution.py:80
  118.9 1.7 copy-start.1
  121.2 2.9 %copy-start.2 = (f32[512,1536]{1,0:T(8,128)S(1)}, f32[512,1536]{1,0:T(8,128)}, u32[]{:S(2)}) copy-start(f32[512,1536]{1,0:T(8,128)} %copy-done.1) | copy-start | bytes 9437188 | tf_op jit(solution)/shard_map/while
  121.2 2.9 %copy-start.6 = (bf16[1536,80]{1,0:T(8,128)(2,1)S(1)}, bf16[1536,80]{1,0:T(8,128)(2,1)}, u32[]{:S(2)}) copy-start(bf16[1536,80]{1,0:T(8,128)(2,1)} %get-tuple-element.512) | copy-start | bytes 737284 | tf_op jit(solution)/shard_map/while
  129.5 1.7 copy-start.1
  131.8 2.9 %copy-start.2 = (f32[512,1536]{1,0:T(8,128)S(1)}, f32[512,1536]{1,0:T(8,128)}, u32[]{:S(2)}) copy-start(f32[512,1536]{1,0:T(8,128)} %copy-done.1) | copy-start | bytes 9437188 | tf_op jit(solution)/shard_map/while
  131.8 2.9 %copy-start.6 = (bf16[1536,80]{1,0:T(8,128)(2,1)S(1)}, bf16[1536,80]{1,0:T(8,128)(2,1)}, u32[]{:S(2)}) copy-start(bf16[1536,80]{1,0:T(8,128)(2,1)} %get-tuple-element.512) | copy-start | bytes 737284 | tf_op jit(solution)/shard_map/while
  142.4 2.9 %copy-start.2 = (f32[512,1536]{1,0:T(8,128)S(1)}, f32[512,1536]{1,0:T(8,128)}, u32[]{:S(2)}) copy-start(f32[512,1536]{1,0:T(8,128)} %copy-done.1) | copy-start | bytes 9437188 | tf_op jit(solution)/shard_map/while
  142.5 2.9 %copy-start.6 = (bf16[1536,80]{1,0:T(8,128)(2,1)S(1)}, bf16[1536,80]{1,0:T(8,128)(2,1)}, u32[]{:S(2)}) copy-start(bf16[1536,80]{1,0:T(8,128)(2,1)} %get-tuple-element.512) | copy-start | bytes 737284 | tf_op jit(solution)/shard_map/while
  150.0 3.9 %copy-start.7 = (bf16[3,512,80]{2,1,0:T(8,128)(2,1)S(1)}, bf16[3,512,80]{2,1,0:T(8,128)(2,1)}, u32[]{:S(2)}) copy-start(bf16[3,512,80]{2,1,0:T(8,128)(2,1)} %get-tuple-element.478) | copy-start | bytes 737284 | tf_op jit(solution)/shard_map/while
  151.7 1.7 copy-start.3
  153.4 3.5 %copy-start.5 = (bf16[1536,80]{1,0:T(8,128)(2,1)S(1)}, bf16[1536,80]{1,0:T(8,128)(2,1)}, u32[]{:S(2)}) copy-start(bf16[1536,80]{1,0:T(8,128)(2,1)} %get-tuple-element.479) | copy-start | bytes 737284 | tf_op jit(solution)/shard_map/while
  154.0 3.0 %copy-start.4 = (f32[512,1536]{1,0:T(8,128)S(1)}, f32[512,1536]{1,0:T(8,128)}, u32[]{:S(2)}) copy-start(f32[512,1536]{1,0:T(8,128)} %copy-done.3) | copy-start | bytes 9437188 | tf_op jit(solution)/shard_map/while
  159.8 4.0 %copy-start.7 = (bf16[3,512,80]{2,1,0:T(8,128)(2,1)S(1)}, bf16[3,512,80]{2,1,0:T(8,128)(2,1)}, u32[]{:S(2)}) copy-start(bf16[3,512,80]{2,1,0:T(8,128)(2,1)} %get-tuple-element.478) | copy-start | bytes 737284 | tf_op jit(solution)/shard_map/while
  163.2 3.5 %copy-start.5 = (bf16[1536,80]{1,0:T(8,128)(2,1)S(1)}, bf16[1536,80]{1,0:T(8,128)(2,1)}, u32[]{:S(2)}) copy-start(bf16[1536,80]{1,0:T(8,128)(2,1)} %get-tuple-element.479) | copy-start | bytes 737284 | tf_op jit(solution)/shard_map/while
  163.8 2.9 %copy-start.4 = (f32[512,1536]{1,0:T(8,128)S(1)}, f32[512,1536]{1,0:T(8,128)}, u32[]{:S(2)}) copy-start(f32[512,1536]{1,0:T(8,128)} %copy-done.3) | copy-start | bytes 9437188 | tf_op jit(solution)/shard_map/while
  169.5 3.9 %copy-start.7 = (bf16[3,512,80]{2,1,0:T(8,128)(2,1)S(1)}, bf16[3,512,80]{2,1,0:T(8,128)(2,1)}, u32[]{:S(2)}) copy-start(bf16[3,512,80]{2,1,0:T(8,128)(2,1)} %get-tuple-element.478) | copy-start | bytes 737284 | tf_op jit(solution)/shard_map/while
  172.9 3.5 %copy-start.5 = (bf16[1536,80]{1,0:T(8,128)(2,1)S(1)}, bf16[1536,80]{1,0:T(8,128)(2,1)}, u32[]{:S(2)}) copy-start(bf16[1536,80]{1,0:T(8,128)(2,1)} %get-tuple-element.479) | copy-start | bytes 737284 | tf_op jit(solution)/shard_map/while
  173.5 2.9 %copy-start.4 = (f32[512,1536]{1,0:T(8,128)S(1)}, f32[512,1536]{1,0:T(8,128)}, u32[]{:S(2)}) copy-start(f32[512,1536]{1,0:T(8,128)} %copy-done.3) | copy-start | bytes 9437188 | tf_op jit(solution)/shard_map/while
  179.2 6.5 %copy-start.9 = (bf16[1536,1,80]{0,2,1:T(8,128)(2,1)S(1)}, bf16[1536,1,80]{0,2,1:T(8,128)(2,1)}, u32[]{:S(2)}) copy-start(bf16[1536,1,80]{0,2,1:T(8,128)(2,1)} %get-tuple-element.331) | copy-start | bytes 737284
  182.1 16.1 %all-to-all-start.7 = ((bf16[1536,1,2,80]{3,2,1,0:T(2,128)(2,1)}), bf16[1536,1,2,80]{3,2,1,0:T(2,128)(2,1)S(1)}, u32[]{:S(2)}, u32[]{:S(2)}) async-start(bf16[1536,1,2,80]{3,2,1,0:T(2,128)(2,1)} %copy.137), calls=%async_computation.7 | async-start | bytes 1572864 | tf_op jit(solution)/shard_map/all_to_all | solution.py:103
  198.2 17.7 %all-to-all-start.6 = ((bf16[1536,1,2,80]{3,2,1,0:T(2,128)(2,1)}), bf16[1536,1,2,80]{3,2,1,0:T(2,128)(2,1)S(1)}, u32[]{:S(2)}, u32[]{:S(2)}) async-start(bf16[1536,1,2,80]{3,2,1,0:T(2,128)(2,1)} %copy.135), calls=%async_computation.6 | async-start | bytes 1572864 | tf_op jit(solution)/shard_map/all_to_all | solution.py:102
  201.8 67.9 %all-reduce.2.cloned.1.call-start = ((), (), s32[]{:S(2)}) async-start(), calls=%async_computation.11 | async-start | bytes 3276800 | tf_op jit(solution)/shard_map/psum | solution.py:114
  215.9 16.1 %all-to-all-start.5 = ((bf16[1536,1,2,80]{3,2,1,0:T(2,128)(2,1)}), bf16[1536,1,2,80]{3,2,1,0:T(2,128)(2,1)S(1)}, u32[]{:S(2)}, u32[]{:S(2)}) async-start(bf16[1536,1,2,80]{3,2,1,0:T(2,128)(2,1)} %copy.132), calls=%async_computation.5 | async-start | bytes 1572864 | tf_op jit(solution)/shard_map/all_to_all | solution.py:101
  (3 other events, 5.2 us)
Sparse Core Ops, SparseCore 0:
  9.6 68.3 all-gather.1
  80.2 113.6 reduce-scatter.1
  205.8 63.8 all-reduce.1
where the time goes:
time: 281 us; the launch traced here: 279 us
  waiting for transfers between devices  103 us (37%)
  local copies, waits for them, and re-layouts  67.1 us (24%)
  matrix products  54.1 us (19%)
  starting transfers between devices  33 us (12%)
  between operations  14 us (5%)
  other arithmetic  7.03 us (3%)
    psum x1, waiting for transfers between devices, body(): d_weight = lax.psum(partial_rows, 'seq')  35.8 us
    unnamed x22, local copies, waits for them, and re-layouts  23.1 us
    dot_general x6, matrix products, one_block(): lax.dot_general(probs_low, dout_block, contract_first, preferred_element_...  16.9 us
    all_gather x1, waiting for transfers between devices, body(): lax.all_gather(w_out, 'dp', axis=0, tiled=True)  16.2 us
    while x42, local copies, waits for them, and re-layouts  10.7 us
    all_to_all x1, waiting for transfers between devices, body(): lax.all_to_all(values_heads, 'seq', split_axis=0, concat_axis=1, tiled=True)  10.6 us
    all_to_all x1, waiting for transfers between devices, body(): lax.all_to_all(keys_heads, 'seq', split_axis=0, concat_axis=1, tiled=True)  10.5 us
    dot_general x6, matrix products, one_block(): lax.dot_general(query_block, keys_h, contract_last, preferred_element_typ...  9.55 us
  transfers between devices with their start and end apart: 11, of which 10 were waited for; matrix products, arithmetic and copies ran while one was open for 38% of the time, Pallas kernels for 0%

commit v1 on v0

--- a/solution.py
+++ b/solution.py
@@ -111,7 +111,9 @@
         scatter_dimension=0,
         tiled=True,
     )
-    d_weight = lax.psum(partial_rows, "seq")
+    d_weight = partial_rows
+    for hop in (1, 2, 4):
+        d_weight = d_weight + lax.ppermute(d_weight, "seq", [(dev, dev ^ hop) for dev in range(8)])
     shape_out = (1, tok_rows, features)
     return (
         query_back.reshape(shape_out),

time: 281 us -> 365 us (1.30)
  waiting for transfers between devices: 103 us -> 170 us
  other arithmetic: 7.03 us -> 15.1 us
    reduce_scatter x1, waiting for transfers between devices: 0.02 us -> 77.5 us  [body(): lax.psum_scatter(lax.dot_general(attn_rows, grad_y, contract_first, prefe...]
    psum x1 -> x0, waiting for transfers between devices: 35.8 us -> none  [body(): d_weight = lax.psum(partial_rows, 'seq')]
    all_to_all x1, waiting for transfers between devices: 10.6 us -> 37.2 us  [body(): lax.all_to_all(values_heads, 'seq', split_axis=0, concat_axis=1, tiled=True)]
    add x0 -> x3, other arithmetic: none -> 9.8 us  [body(): d_weight + lax.ppermute(d_weight, 'seq', [(dev, dev ^ hop) for dev in ran...]
    ppermute x0 -> x3, waiting for transfers between devices: none -> 5.6 us  [body(): lax.ppermute(d_weight, 'seq', [(dev, dev ^ hop) for dev in range(8)])]
    all_gather x1, waiting for transfers between devices: 16.2 us -> 11 us  [body(): lax.all_gather(w_out, 'dp', axis=0, tiled=True)]
    all_to_all x1, waiting for transfers between devices: 7.23 us -> 2.7 us  [body(): lax.all_to_all(split_heads(keys), 'seq', split_axis=1, concat_axis=0, til...]
    all_to_all x1, waiting for transfers between devices: 1.89 us -> 5.68 us  [body(): lax.all_to_all(split_heads(query), 'seq', split_axis=1, concat_axis=0, ti...]
  transfers between devices with their start and end apart: 11 -> 13, of which waited for: 10 -> 11; matrix products, arithmetic and copies ran while one was open for 38% -> 31% of each run, Pallas kernels for 0% -> 0%
where the time goes in v1:
time: 365 us; the launch traced here: 363 us
  waiting for transfers between devices  170 us (47%)
  local copies, waits for them, and re-layouts  69.7 us (19%)
  matrix products  57.7 us (16%)
  starting transfers between devices  35.3 us (10%)
  other arithmetic  15.1 us (4%)
  between operations  14.3 us (4%)
    reduce_scatter x1, waiting for transfers between devices, body(): lax.psum_scatter(lax.dot_general(attn_rows, grad_y, contract_first, prefe...  77.5 us
    all_to_all x1, waiting for transfers between devices, body(): lax.all_to_all(values_heads, 'seq', split_axis=0, concat_axis=1, tiled=True)  37.2 us
    unnamed x29, local copies, waits for them, and re-layouts  23.5 us
    dot_general x6, matrix products, one_block(): lax.dot_general(probs_low, dout_block, contract_first, preferred_element_...  16.9 us
    all_gather x1, waiting for transfers between devices, body(): lax.all_gather(w_out, 'dp', axis=0, tiled=True)  11 us
    dot_general x6, matrix products, one_block(): lax.dot_general(dout_block, values_h, contract_last, preferred_element_ty...  10.7 us
    while x30, local copies, waits for them, and re-layouts  10.1 us
    add x3, other arithmetic, body(): d_weight + lax.ppermute(d_weight, 'seq', [(dev, dev ^ hop) for dev in ran...  9.8 us
  transfers between devices with their start and end apart: 13, of which 11 were waited for; matrix products, arithmetic and copies ran while one was open for 31% of the time, Pallas kernels for 0%

profile of v1, /device:TPU:0, one launch (start us, length us, event | category | flops | bytes accessed | tf_op | source)
XLA Modules:
  0.0 362.8 jit_solution(16047036751451566151)
XLA Ops:
  8.2 4.8 %convolution_multiply_fusion.2 = f32[1280,1280]{1,0:T(8,128)} fusion(bf16[1,192,1280]{2,1,0:T(8,128)(2,1)} %param.13, bf16[1,192,1280]{2,1,0:T(8,128)(2,1)S(1)} %copy-done), kind=kOutput, calls=%fused_computation.54 | convolution fusion | flops 630784000 | bytes 7536640 | tf_op jit(solution)/shard_map/dot_general | solution.py:108
  15.1 5.2 %all-to-all-start = ((bf16[192,8,2,80]{0,3,2,1:T(8,128)(2,1)}), bf16[192,8,2,80]{0,3,2,1:T(8,128)(2,1)S(1)}, u32[]{:S(2)}, u32[]{:S(2)}) async-start(bf16[192,8,2,80]{0,3,2,1:T(8,128)(2,1)} %bitcast), calls=%async_computation | async-start | bytes 1310720 | tf_op jit(solution)/shard_map/all_to_all | solution.py:76
  25.8 5.7 %all-to-all-done = bf16[192,8,2,80]{0,3,2,1:T(8,128)(2,1)S(1)} async-done(((bf16[192,8,2,80]{0,3,2,1:T(8,128)(2,1)}), bf16[192,8,2,80]{0,3,2,1:T(8,128)(2,1)S(1)}, u32[]{:S(2)}, u32[]{:S(2)}) %all-to-all-start) | async-done | bytes 491552 | tf_op jit(solution)/shard_map/all_to_all | solution.py:76
  32.3 3.5 all-to-all-start.1
  44.2 2.7 all-to-all-done.1
  46.9 4.2 %all-to-all-start.3 = ((bf16[192,8,2,80]{0,3,2,1:T(8,128)(2,1)}), bf16[192,8,2,80]{0,3,2,1:T(8,128)(2,1)}, u32[]{:S(2)}, u32[]{:S(2)}) async-start(bf16[192,8,2,80]{0,3,2,1:T(8,128)(2,1)} %bitcast.13), calls=%async_computation.3 | async-start | bytes 1310720 | tf_op jit(solution)/shard_map/all_to_all | solution.py:78
  56.0 6.2 %all-to-all-done.3 = bf16[192,8,2,80]{0,3,2,1:T(8,128)(2,1)} async-done(((bf16[192,8,2,80]{0,3,2,1:T(8,128)(2,1)}), bf16[192,8,2,80]{0,3,2,1:T(8,128)(2,1)}, u32[]{:S(2)}, u32[]{:S(2)}) %all-to-all-start.3) | async-done | bytes 491552 | tf_op jit(solution)/shard_map/all_to_all | solution.py:78
  66.9 11.0 %all-gather.2.cloned.1.call-done = bf16[1280,1280]{1,0:T(8,128)(2,1)} async-done(((bf16[320,1280]{1,0:T(8,128)(2,1)}), bf16[1280,1280]{1,0:T(8,128)(2,1)}) %all-gather.2.cloned.1.call-update) | async-done | bytes 3276816 | tf_op jit(solution)/shard_map/all_gather | solution.py:67
  77.9 3.9 %convolution_convert_fusion.2 = bf16[192,1280]{1,0:T(8,128)(2,1)} fusion(bf16[1280,1280]{1,0:T(8,128)(2,1)} %all-gather.2.cloned.1.call-done, bf16[1,192,1280]{2,1,0:T(8,128)(2,1)S(1)} %copy-done), kind=kOutput, calls=%fused_computation.55 | convolution fusion | flops 629391360 | bytes 4259840 | tf_op jit(solution)/shard_map/dot_general | solution.py:65
  84.0 4.2 %all-to-all-start.2 = ((bf16[192,8,2,80]{0,3,2,1:T(8,128)(2,1)}), bf16[192,8,2,80]{0,3,2,1:T(8,128)(2,1)}, u32[]{:S(2)}, u32[]{:S(2)}) async-start(bf16[192,8,2,80]{0,3,2,1:T(8,128)(2,1)} %bitcast.194), calls=%async_computation.2 | async-start | bytes 1310720 | tf_op jit(solution)/shard_map/all_to_all | solution.py:79
  94.9 4.4 %all-to-all-done.2 = bf16[192,8,2,80]{0,3,2,1:T(8,128)(2,1)} async-done(((bf16[192,8,2,80]{0,3,2,1:T(8,128)(2,1)}), bf16[192,8,2,80]{0,3,2,1:T(8,128)(2,1)}, u32[]{:S(2)}, u32[]{:S(2)}) %all-to-all-start.2) | async-done | bytes 491552 | tf_op jit(solution)/shard_map/all_to_all | solution.py:79
  99.3 4.4 %all-to-all-start.4 = ((bf16[192,8,2,80]{0,3,2,1:T(8,128)(2,1)}), bf16[192,8,2,80]{0,3,2,1:T(8,128)(2,1)}, u32[]{:S(2)}, u32[]{:S(2)}) async-start(bf16[192,8,2,80]{0,3,2,1:T(8,128)(2,1)} %bitcast.190), calls=%async_computation.4 | async-start | bytes 1310720 | tf_op jit(solution)/shard_map/all_to_all | solution.py:80
  111.1 3.5 all-to-all-done.4
  116.4 77.5 %reduce-scatter.2.cloned.1.call-done = f32[320,1280]{1,0:T(8,128)} async-done(((f32[1280,1280]{1,0:T(8,128)}), f32[320,1280]{1,0:T(8,128)}) %reduce-scatter.2.cloned.1.call-update) | async-done | bytes 1638416 | tf_op jit(solution)/shard_map/reduce_scatter | solution.py:107
  193.9 31.5 %while.30 = (s32[]{:T(128)}, f32[1536,80]{0,1:T(8,128)S(1)}, f32[1536,80]{0,1:T(8,128)S(1)}, bf16[3,512,80]{1,2,0:T(8,128)(2,1)S(1)}, bf16[3,512,80]{2,1,0:T(8,1...) while((s32[]{:T(128)}, f32[1536,80]{0,1:T(8,128)S(1)}, ...), condition=%wide.region_4.5_spmd.clone, body=%wide.region_1.4_spmd.clone.sunk | while | flops 638328320 | bytes 46932176 | solution.py:49
  197.7 2.8 convolution_add_fusion.9
  208.2 2.8 convolution_add_fusion.9
  218.8 2.8 convolution_add_fusion.9
  227.5 3.3 add.45
  232.2 31.4 %while.31 = (s32[]{:T(128)}, f32[1536,80]{0,1:T(8,128)S(1)}, f32[1536,80]{0,1:T(8,128)S(1)}, bf16[3,512,80]{1,2,0:T(8,128)(2,1)S(1)}, bf16[3,512,80]{2,1,0:T(8,1...) while((s32[]{:T(128)}, f32[1536,80]{0,1:T(8,128)S(1)}, ...), condition=%wide.region_8.9_spmd.clone, body=%wide.region_5.8_spmd.clone.sunk | while | flops 638328320 | bytes 45949108 | solution.py:49
  236.0 2.8 convolution_add_fusion.11
  246.5 2.8 convolution_add_fusion.11
  257.0 2.8 convolution_add_fusion.11
  263.7 5.6 %collective-permute-done.1 = f32[320,1280]{1,0:T(8,128)} collective-permute-done((f32[320,1280]{1,0:T(8,128)}, f32[320,1280]{1,0:T(8,128)}, u32[]{:S(2)}, u32[]{:S(2)}) %collective-permute-start.1) | collective-permute-done | bytes 1638432 | tf_op jit(solution)/shard_map/ppermute | solution.py:116
  269.3 3.3 add.46
  275.9 3.5 all-to-all-start.7
  281.4 37.2 %all-to-all-done.7 = bf16[1536,1,2,80]{3,2,1,0:T(2,128)(2,1)S(1)} async-done(((bf16[1536,1,2,80]{3,2,1,0:T(2,128)(2,1)}), bf16[1536,1,2,80]{3,2,1,0:T(2,128)(2,1)S(1)}, u32[]{:S(2)}, u32[]{:S(2)}) %all-to-all-start.7) | async-done | bytes 491552 | tf_op jit(solution)/shard_map/all_to_all | solution.py:103
  318.5 3.6 %all-to-all-start.6 = ((bf16[1536,1,2,80]{3,2,1,0:T(2,128)(2,1)}), bf16[1536,1,2,80]{3,2,1,0:T(2,128)(2,1)S(1)}, u32[]{:S(2)}, u32[]{:S(2)}) async-start(bf16[1536,1,2,80]{3,2,1,0:T(2,128)(2,1)} %copy.135), calls=%async_computation.6 | async-start | bytes 1572864 | tf_op jit(solution)/shard_map/all_to_all | solution.py:102
  325.2 9.6 %all-to-all-done.6 = bf16[1536,1,2,80]{3,2,1,0:T(2,128)(2,1)S(1)} async-done(((bf16[1536,1,2,80]{3,2,1,0:T(2,128)(2,1)}), bf16[1536,1,2,80]{3,2,1,0:T(2,128)(2,1)S(1)}, u32[]{:S(2)}, u32[]{:S(2)}) %all-to-all-start.6) | async-done | bytes 491552 | tf_op jit(solution)/shard_map/all_to_all | solution.py:102
  334.7 3.5 all-to-all-start.5
  344.5 6.2 %all-to-all-done.5 = bf16[1536,1,2,80]{3,2,1,0:T(2,128)(2,1)S(1)} async-done(((bf16[1536,1,2,80]{3,2,1,0:T(2,128)(2,1)}), bf16[1536,1,2,80]{3,2,1,0:T(2,128)(2,1)S(1)}, u32[]{:S(2)}, u32[]{:S(2)}) %all-to-all-start.5) | async-done | bytes 491552 | tf_op jit(solution)/shard_map/all_to_all | solution.py:101
  352.7 3.3 add.47
  (151 shorter events, 110.7 us)
Async XLA Ops:
  7.2 70.7 %all-gather.2.cloned.1.call-start = ((), (), s32[]{:S(2)}) async-start(), calls=%async_computation.9 | async-start | bytes 4096000 | tf_op jit(solution)/shard_map/all_gather | solution.py:67
  7.9 186.0 %reduce-scatter.2.cloned.1.call-start = ((), (), s32[]{:S(2)}) async-start(), calls=%async_computation.10 | async-start | bytes 8192000 | tf_op jit(solution)/shard_map/reduce_scatter | solution.py:107
  13.0 7.3 %copy-start.7 = (bf16[1,192,1280]{2,1,0:T(8,128)(2,1)S(1)}, bf16[1,192,1280]{2,1,0:T(8,128)(2,1)}, u32[]{:S(2)}) copy-start(bf16[1,192,1280]{2,1,0:T(8,128)(2,1)} %param.13) | copy-start | bytes 1474564
  15.1 16.3 %all-to-all-start = ((bf16[192,8,2,80]{0,3,2,1:T(8,128)(2,1)}), bf16[192,8,2,80]{0,3,2,1:T(8,128)(2,1)S(1)}, u32[]{:S(2)}, u32[]{:S(2)}) async-start(bf16[192,8,2,80]{0,3,2,1:T(8,128)(2,1)} %bitcast), calls=%async_computation | async-start | bytes 1310720 | tf_op jit(solution)/shard_map/all_to_all | solution.py:76
  32.3 14.6 %all-to-all-start.1 = ((bf16[192,8,2,80]{0,3,2,1:T(8,128)(2,1)}), bf16[192,8,2,80]{0,3,2,1:T(8,128)(2,1)S(1)}, u32[]{:S(2)}, u32[]{:S(2)}) async-start(bf16[192,8,2,80]{0,3,2,1:T(8,128)(2,1)} %bitcast.193), calls=%async_computation.1 | async-start | bytes 1310720 | tf_op jit(solution)/shard_map/all_to_all | solution.py:77
  46.9 15.3 %all-to-all-start.3 = ((bf16[192,8,2,80]{0,3,2,1:T(8,128)(2,1)}), bf16[192,8,2,80]{0,3,2,1:T(8,128)(2,1)}, u32[]{:S(2)}, u32[]{:S(2)}) async-start(bf16[192,8,2,80]{0,3,2,1:T(8,128)(2,1)} %bitcast.13), calls=%async_computation.3 | async-start | bytes 1310720 | tf_op jit(solution)/shard_map/all_to_all | solution.py:78
  84.0 15.4 %all-to-all-start.2 = ((bf16[192,8,2,80]{0,3,2,1:T(8,128)(2,1)}), bf16[192,8,2,80]{0,3,2,1:T(8,128)(2,1)}, u32[]{:S(2)}, u32[]{:S(2)}) async-start(bf16[192,8,2,80]{0,3,2,1:T(8,128)(2,1)} %bitcast.194), calls=%async_computation.2 | async-start | bytes 1310720 | tf_op jit(solution)/shard_map/all_to_all | solution.py:79
  99.3 15.3 %all-to-all-start.4 = ((bf16[192,8,2,80]{0,3,2,1:T(8,128)(2,1)}), bf16[192,8,2,80]{0,3,2,1:T(8,128)(2,1)}, u32[]{:S(2)}, u32[]{:S(2)}) async-start(bf16[192,8,2,80]{0,3,2,1:T(8,128)(2,1)} %bitcast.190), calls=%async_computation.4 | async-start | bytes 1310720 | tf_op jit(solution)/shard_map/all_to_all | solution.py:80
  193.9 33.6 %collective-permute-start = (f32[320,1280]{1,0:T(8,128)}, f32[320,1280]{1,0:T(8,128)}, u32[]{:S(2)}, u32[]{:S(2)}) collective-permute-start(f32[320,1280]{1,0:T(8,128)} %reduce-scatter.2.cloned.1.call-done), channel_id=1, source_target_pairs={{0,4},{4,0},{8,12},{12,8},{16,20},{20,16},{24,28},{28,24},{1,5},{5... | collective-permute-start | bytes 4915208 | tf_op jit(solution)/shard_map/ppermute | solution.py:116
  195.5 1.6 copy-start.1
  197.7 2.9 copy-start.2
  197.7 2.9 copy-start.6
  206.0 1.6 copy-start.1
  208.2 2.9 copy-start.2
  208.2 2.9 copy-start.6
  216.5 1.6 copy-start.1
  218.7 2.9 copy-start.2
  218.7 2.9 copy-start.6
  225.5 6.7 %copy-start.9 = (bf16[3,512,80]{1,2,0:T(8,128)(2,1)}, bf16[3,512,80]{1,2,0:T(8,128)(2,1)S(1)}, u32[]{:S(2)}) copy-start(bf16[3,512,80]{1,2,0:T(8,128)(2,1)S(1)} %get-tuple-element.102) | copy-start | bytes 737284
  225.5 6.8 %copy-start.5 = (bf16[1536,80]{1,0:T(8,128)(2,1)S(1)}, bf16[1536,80]{1,0:T(8,128)(2,1)}, u32[]{:S(2)}) copy-start(bf16[1536,80]{1,0:T(8,128)(2,1)} %copy.130) | copy-start | bytes 737284
  230.7 38.5 %collective-permute-start.1 = (f32[320,1280]{1,0:T(8,128)}, f32[320,1280]{1,0:T(8,128)}, u32[]{:S(2)}, u32[]{:S(2)}) collective-permute-start(f32[320,1280]{1,0:T(8,128)} %add.45), channel_id=1, source_target_pairs={{0,8},{4,12},{8,0},{12,4},{16,24},{20,28},{24,16},{28,20},{1,9},{5... | collective-permute-start | bytes 4915208 | tf_op jit(solution)/shard_map/ppermute | solution.py:116
  233.8 1.6 copy-start.3
  236.0 2.9 copy-start.4
  244.3 1.6 copy-start.3
  246.5 2.9 copy-start.4
  254.7 1.6 copy-start.3
  256.9 2.9 copy-start.4
  272.5 80.2 %collective-permute-start.2 = (f32[320,1280]{1,0:T(8,128)}, f32[320,1280]{1,0:T(8,128)}, u32[]{:S(2)}, u32[]{:S(2)}) collective-permute-start(f32[320,1280]{1,0:T(8,128)} %add.46), channel_id=1, source_target_pairs={{0,16},{4,20},{8,24},{12,28},{16,0},{20,4},{24,8},{28,12},{1,17},{... | collective-permute-start | bytes 4915208 | tf_op jit(solution)/shard_map/ppermute | solution.py:116
  274.1 48.1 %copy-start.10 = (bf16[3,512,80]{1,2,0:T(8,128)(2,1)S(1)}, bf16[3,512,80]{1,2,0:T(8,128)(2,1)}, u32[]{:S(2)}) copy-start(bf16[3,512,80]{1,2,0:T(8,128)(2,1)} %copy-done.9) | copy-start | bytes 737284
  275.9 42.6 %all-to-all-start.7 = ((bf16[1536,1,2,80]{3,2,1,0:T(2,128)(2,1)}), bf16[1536,1,2,80]{3,2,1,0:T(2,128)(2,1)S(1)}, u32[]{:S(2)}, u32[]{:S(2)}) async-start(bf16[1536,1,2,80]{3,2,1,0:T(2,128)(2,1)} %copy.137), calls=%async_computation.7 | async-start | bytes 1572864 | tf_op jit(solution)/shard_map/all_to_all | solution.py:103
  318.5 16.2 %all-to-all-start.6 = ((bf16[1536,1,2,80]{3,2,1,0:T(2,128)(2,1)}), bf16[1536,1,2,80]{3,2,1,0:T(2,128)(2,1)S(1)}, u32[]{:S(2)}, u32[]{:S(2)}) async-start(bf16[1536,1,2,80]{3,2,1,0:T(2,128)(2,1)} %copy.135), calls=%async_computation.6 | async-start | bytes 1572864 | tf_op jit(solution)/shard_map/all_to_all | solution.py:102
  334.7 16.1 %all-to-all-start.5 = ((bf16[1536,1,2,80]{3,2,1,0:T(2,128)(2,1)}), bf16[1536,1,2,80]{3,2,1,0:T(2,128)(2,1)S(1)}, u32[]{:S(2)}, u32[]{:S(2)}) async-start(bf16[1536,1,2,80]{3,2,1,0:T(2,128)(2,1)} %copy.132), calls=%async_computation.5 | async-start | bytes 1572864 | tf_op jit(solution)/shard_map/all_to_all | solution.py:101
  (3 other events, 2.9 us)
Sparse Core Ops, SparseCore 0:
  9.6 68.3 all-gather.1
  80.2 113.6 reduce-scatter.1
